TPU v7x, 128 devices: a whole 4x4x4 slice. The times are simulated.
128 devices in a mesh: row: 8 (over y, x_lo), col: 16 (over z, x_hi, core).
Axes of the slice: x: 4 (x_hi: 2, x_lo: 2; x = x_hi * 2 + x_lo), y: 4, z: 4, core: 2. Of those that a mesh axis runs over, the one named last changes fastest.
Arguments:
- pair: bfloat16 [256, 256, 128], P('row', 'col'), may hold values from -6 to 6
- cotangent: bfloat16 [256, 256, 128], P('row', 'col'), may hold values from -6 to 6
- token_mask: int32 [256], replicated, may hold values 0 or 1
- out_in_proj: bfloat16 [128, 640], replicated, may hold values from -0.5 to 0.5
- out_out_proj: bfloat16 [128, 128], replicated, may hold values from -0.5 to 0.5
- in_in_proj: bfloat16 [128, 640], replicated, may hold values from -0.5 to 0.5
- in_out_proj: bfloat16 [128, 128], replicated, may hold values from -0.5 to 0.5
Outputs:
- updated_pair: bfloat16 [256, 256, 128], P('row', 'col')
- pair_grad: bfloat16 [256, 256, 128], P('row', 'col')
- out_in_grad: float32 [128, 640], replicated
- out_out_grad: float32 [128, 128], replicated
- in_in_grad: float32 [128, 640], replicated
- in_out_grad: float32 [128, 128], replicated
All inputs are finite; a program needn't handle non-finite values.
Results may differ from a plain program's by a relative error of at most 0.012.
Values may be sent and summed in bfloat16 or wider, within the bound.
A program may use at most 128 MiB of HBM per device.

v0:
```python
import jax
import jax.numpy as jnp
from jax import lax
from jax.sharding import PartitionSpec as P

H = 128
EPSILON = 1e-05


def shortened(array):
    return jax.tree.map(lambda a: a.astype(jnp.bfloat16) if a.dtype == jnp.float32 else a, array)


def from_everyone(array, axis):
    copies = jnp.broadcast_to(array, (lax.axis_size(axis), *array.shape))
    return lax.all_to_all(copies, axis, split_axis=0, concat_axis=0, tiled=True)


def in_order(tiles, dim):
    shape = list(tiles.shape[1:])
    shape[dim] *= tiles.shape[0]
    return jnp.moveaxis(tiles, 0, dim).reshape(shape)


def collect(array, axis, dim):
    tiles = from_everyone(array, axis)
    return in_order(tiles, dim)


def normalize(values):
    centre = jnp.mean(values, axis=-1, keepdims=True)
    shifted = values - centre
    spread = jnp.mean(shifted * shifted, axis=-1, keepdims=True)
    return shifted * lax.rsqrt(spread + EPSILON)


def gating(projected, pair_mask):
    left_value = projected[..., :H]
    left_gate = projected[..., H : 2 * H]
    right_value = projected[..., 2 * H : 3 * H]
    right_gate = projected[..., 3 * H : 4 * H]
    left_full = jax.nn.sigmoid(left_gate) * left_value * pair_mask
    right_full = jax.nn.sigmoid(right_gate) * right_value * pair_mask
    return (left_full, right_full, jax.nn.sigmoid(projected[..., 4 * H :]))


def cols_of(tiles):
    return jax.tree.map(
        lambda part, own: part.astype(own.dtype),
        lax.all_gather(shortened(tiles), "col", axis=1, tiled=True),
        tiles,
    )


def rows_of(tiles):
    return jax.tree.map(
        lambda part, own: part.astype(own.dtype),
        jax.tree.map(lambda part: collect(part, "row", 0), shortened(tiles)),
        tiles,
    )


def to_row_blocks(panel):
    return lax.all_to_all(panel, "col", split_axis=0, concat_axis=1, tiled=True)


def to_col_blocks(panel):
    return lax.all_to_all(panel, "row", split_axis=1, concat_axis=0, tiled=True)


def outgoing_sum(left_tile, right_tile):
    row_panels = rows_of((left_tile, right_tile))
    left_panel = cols_of(left_tile)
    right_rows = to_row_blocks(row_panels[1])
    total = jnp.einsum("ikh,jkh->ijh", left_panel, right_rows, preferred_element_type=jnp.float32)
    return (total, row_panels)


def incoming_sum(left_tile, right_tile):
    col_panels = cols_of((left_tile, right_tile))
    right_all = rows_of(right_tile)
    left_cols = to_col_blocks(col_panels[0])
    total = jnp.einsum("kih,kjh->ijh", left_cols, right_all, preferred_element_type=jnp.float32)
    return (total, col_panels)


def outgoing_grads(tri_grad, row_panels):
    grad_cols = cols_of(tri_grad)
    grad_rows = to_col_blocks(grad_cols)
    left_grad = jnp.einsum(
        "ijh,jkh->ikh", grad_cols, row_panels[1], preferred_element_type=jnp.float32
    )
    right_grad = jnp.einsum(
        "ijh,ikh->jkh", grad_rows, row_panels[0], preferred_element_type=jnp.float32
    )
    return (left_grad, right_grad)


def incoming_grads(tri_grad, col_panels):
    grad_rows = rows_of(tri_grad)
    grad_cols = to_row_blocks(grad_rows)
    left_grad = jnp.einsum(
        "ijh,kjh->kih", grad_cols, col_panels[1], preferred_element_type=jnp.float32
    )
    right_grad = jnp.einsum(
        "kih,ijh->kjh", col_panels[0], grad_rows, preferred_element_type=jnp.float32
    )
    return (left_grad, right_grad)


def forward(pair_in, pair_mask, w_in, w_out, outgoing):
    pair_wide = pair_in.astype(jnp.float32)
    normed = normalize(pair_wide).astype(jnp.bfloat16)
    projected = jnp.dot(normed, w_in, preferred_element_type=jnp.float32)
    left_full, right_full, gate = gating(projected, pair_mask)
    left_tile = left_full.astype(jnp.bfloat16)
    right_tile = right_full.astype(jnp.bfloat16)
    if outgoing:
        triangle_sum, panels = outgoing_sum(left_tile, right_tile)
    else:
        triangle_sum, panels = incoming_sum(left_tile, right_tile)
    tri_normed = normalize(triangle_sum).astype(jnp.bfloat16)
    lifted = jnp.dot(tri_normed, w_out, preferred_element_type=jnp.float32)
    result = (pair_wide + gate * lifted).astype(jnp.bfloat16)
    saved = (pair_wide, normed, projected, gate, triangle_sum, tri_normed, lifted, panels)
    return (result, saved)


def backward(cotan, saved, pair_mask, w_in, w_out, outgoing):
    pair_wide, normed, projected, gate, triangle_sum, tri_normed, lifted, panels = saved
    cot_wide = cotan.astype(jnp.float32)
    lift_grad = gate * cot_wide
    gate_grad = lifted * cot_wide
    out_grad = jnp.einsum(
        "ijh,ijc->hc", tri_normed.astype(jnp.float32), lift_grad, precision=lax.Precision.HIGHEST
    )
    normed_tri_grad = jnp.dot(
        lift_grad, w_out.astype(jnp.float32).T, precision=lax.Precision.HIGHEST
    )
    tri_grad = jax.vjp(normalize, triangle_sum)[1](normed_tri_grad)[0].astype(jnp.bfloat16)
    if outgoing:
        left_grad, right_grad = outgoing_grads(tri_grad, panels)
    else:
        left_grad, right_grad = incoming_grads(tri_grad, panels)
    gate_vjp = jax.vjp(lambda values: gating(values, pair_mask), projected)[1]
    proj_grad = gate_vjp((left_grad, right_grad, gate_grad))[0]
    in_grad = jnp.einsum(
        "ijc,ijq->cq", normed.astype(jnp.float32), proj_grad, precision=lax.Precision.HIGHEST
    )
    normed_grad = jnp.dot(proj_grad, w_in.astype(jnp.float32).T, precision=lax.Precision.HIGHEST)
    pair_grad = (cot_wide + jax.vjp(normalize, pair_wide)[1](normed_grad)[0]).astype(jnp.bfloat16)
    return (pair_grad, in_grad, out_grad)


def local(pair, cotangent, token_mask, out_in_proj, out_out_proj, in_in_proj, in_out_proj):
    row_tile = pair.shape[0]
    col_tile = pair.shape[1]
    row_flags = lax.dynamic_slice_in_dim(
        token_mask, lax.axis_index("row") * row_tile, row_tile, 0
    ).astype(jnp.float32)
    col_flags = lax.dynamic_slice_in_dim(
        token_mask, lax.axis_index("col") * col_tile, col_tile, 0
    ).astype(jnp.float32)
    pair_mask = (row_flags[:, None] * col_flags[None, :])[:, :, None]
    middle, saved_out = forward(pair, pair_mask, out_in_proj, out_out_proj, True)
    updated, saved_in = forward(middle, pair_mask, in_in_proj, in_out_proj, False)
    middle_grad, in_in_part, in_out_part = backward(
        cotangent, saved_in, pair_mask, in_in_proj, in_out_proj, False
    )
    pair_grad, out_in_part, out_out_part = backward(
        middle_grad, saved_out, pair_mask, out_in_proj, out_out_proj, True
    )
    totals = lax.psum((out_in_part, out_out_part, in_in_part, in_out_part), ("row", "col"))
    tokens_all = row_tile * lax.axis_size("row")
    return (
        updated,
        pair_grad,
        totals[0] / tokens_all,
        totals[1] / tokens_all,
        totals[2] / tokens_all,
        totals[3] / tokens_all,
    )


def solution(mesh):
    return jax.shard_map(
        local,
        mesh=mesh,
        in_specs=(P("row", "col", None), P("row", "col", None), P(), P(), P(), P(), P()),
        out_specs=(P("row", "col", None), P("row", "col", None), P(), P(), P(), P()),
        check_vma=False,
    )
```

profile of v0, /device:TPU:1, one launch (start us, length us, event | category | flops | bytes accessed | tf_op | source)
XLA Modules:
  0.0 564.3 jit_solution(1086619950908574980)
XLA Ops:
  10.0 1.1 fusion.10
  11.9 1.4 fusion.53
  14.3 22.1 %all_to_all.92 = bf16[8,32,16,128]{3,2,1,0:T(8,128)(2,1)S(1)} all-to-all(bf16[8,32,16,128]{3,2,1,0:T(8,128)(2,1)S(1)} %broadcast_in_dim.24), channel_id=1, replica_groups=mesh['row'=8,'col'=16] {'row'}, dimensions={0} | all-to-all | bytes 2097152 | tf_op jit(solution)/shard_map/all_to_all | solution.py:16
  36.4 31.5 %all_to_all.93 = bf16[256,16,128]{2,1,0:T(8,128)(2,1)S(1)} all-to-all(bf16[256,16,128]{2,1,0:T(8,128)(2,1)S(1)} %bitcast.135), channel_id=1, replica_groups=mesh['row'=8,'col'=16] {'col'}, dimensions={0} | all-to-all | bytes 2097152 | tf_op jit(solution)/shard_map/all_to_all | solution.py:64
  67.9 1.3 copy.219
  69.1 2.7 copy.220
  72.3 15.3 %copy.221 = bf16[32,256,128]{0,1,2:T(8,128)(2,1)} copy(bf16[32,256,128]{2,1,0:T(8,128)(2,1)} %all-gather.5.cloned.1.call-done) | data formatting | bytes 4194304 | tf_op jit(solution)/shard_map/all_gather | solution.py:50
  87.6 6.0 %bitcast_reduce_fusion.1 = (f32[32,16]{0,1:T(8,128)S(1)}, f32[128,16,32]{2,1,0:T(8,128)}) fusion(bf16[16,256,128]{1,0,2:T(8,128)(2,1)} %copy.220, bf16[32,256,128]{0,1,2:T(8,128)(2,1)} %copy.221), kind=kOutput, calls=%fused_computation.7 | convolution fusion | flops 33619456 | bytes 3409920 | tf_op jit(solution)/shard_map/ikh,jkh->ijh/dot_general | solution.py:75
  93.6 1.7 copy.222
  101.4 4.2 all-to-all-start.2
  105.7 40.1 %all-gather.7.cloned.1.call-done = bf16[32,256,128]{2,1,0:T(8,128)(2,1)} async-done(((bf16[32,16,128]{2,1,0:T(8,128)(2,1)}), bf16[32,256,128]{2,1,0:T(8,128)(2,1)}) %all-gather.7.cloned.1.call-update) | async-done | bytes 2097168 | tf_op jit(solution)/shard_map/all_gather | solution.py:50
  145.8 4.3 copy.231
  150.1 4.4 all-to-all-start.3
  155.2 3.0 copy.234
  158.2 24.5 %all-to-all-done.3 = bf16[32,256,128]{2,0,1:T(8,128)(2,1)} async-done(((bf16[32,256,128]{2,0,1:T(8,128)(2,1)}), bf16[32,256,128]{2,0,1:T(8,128)(2,1)}, u32[]{:S(2)}, u32[]{:S(2)}) %all-to-all-start.3) | async-done | bytes 2097184 | tf_op jit(solution)/shard_map/all_to_all | solution.py:68
  182.6 3.7 copy.233
  186.4 4.9 copy.235
  191.3 3.6 bitcast_reduce_fusion
  194.8 1.7 copy.236
  196.6 2.0 multiply_reduce_fusion.1
  199.0 1.3 fusion.67
  200.4 1.3 add_convert_fusion.1
  201.9 17.9 %all_to_all.94 = bf16[8,32,16,128]{3,2,1,0:T(8,128)(2,1)} all-to-all(bf16[8,32,16,128]{3,2,1,0:T(8,128)(2,1)S(1)} %broadcast_in_dim.28), channel_id=1, replica_groups=mesh['row'=8,'col'=16] {'row'}, dimensions={0} | all-to-all | bytes 2097152 | tf_op jit(solution)/shard_map/all_to_all | solution.py:16
  219.8 6.1 %all-to-all-start.5 = ((bf16[256,16,128]{2,1,0:T(8,128)(2,1)}), bf16[256,16,128]{2,1,0:T(8,128)(2,1)}, u32[]{:S(2)}, u32[]{:S(2)}) async-start(bf16[256,16,128]{2,1,0:T(8,128)(2,1)} %bitcast.137), calls=%async_computation.5 | async-start | bytes 2097152 | tf_op jit(solution)/shard_map/all_to_all | solution.py:64
  225.9 15.2 %copy.246 = bf16[32,256,128]{0,1,2:T(8,128)(2,1)} copy(bf16[32,256,128]{2,1,0:T(8,128)(2,1)} %all-gather.7.cloned.1.call-done) | data formatting | bytes 4194304 | tf_op jit(solution)/shard_map/all_gather | solution.py:50
  241.2 15.3 %copy.249 = bf16[32,256,128]{0,1,2:T(8,128)(2,1)} copy(bf16[32,256,128]{2,1,0:T(8,128)(2,1)} %all-gather.9.cloned.1.call-done) | data formatting | bytes 4194304 | tf_op jit(solution)/shard_map/all_gather | solution.py:50
  256.5 3.0 copy.245
  259.4 5.9 %fusion.83 = f32[128,16,32]{2,1,0:T(8,128)} fusion(bf16[256,16,128]{0,1,2:T(8,128)(2,1)} %copy.245, bf16[32,256,128]{0,1,2:T(8,128)(2,1)} %copy.246), kind=kOutput, calls=%fused_computation.151 | convolution fusion | flops 33554432 | bytes 3407872 | tf_op jit(solution)/shard_map/kih,ijh->kjh/dot_general | solution.py:105
  265.4 2.3 copy.247
  267.7 2.5 copy.248
  270.2 2.7 copy.250
  272.9 5.9 %fusion.86 = f32[128,32,16]{1,2,0:T(8,128)} fusion(bf16[16,256,128]{1,0,2:T(8,128)(2,1)} %copy.250, bf16[32,256,128]{0,1,2:T(8,128)(2,1)} %copy.249), kind=kOutput, calls=%fused_computation.154 | convolution fusion | flops 33554432 | bytes 3407872 | tf_op jit(solution)/shard_map/ijh,kjh->kih/dot_general | solution.py:102
  278.8 2.4 copy.251
  281.2 2.6 fusion.18
  283.8 1.4 fusion.16
  285.4 1.3 fusion.55
  286.9 2.1 fusion.22
  289.6 2.4 multiply_reduce_fusion
  292.0 1.4 copy.281
  293.4 1.3 multiply_multiply_fusion.1
  294.8 1.4 copy.257
  296.1 1.9 fusion.68
  298.1 1.4 copy.282
  299.5 1.3 negate_multiply_fusion.1
  300.7 1.4 copy.259
  302.1 2.0 add_convert_fusion
  305.2 4.2 all-to-all-start.6
  309.5 42.8 %all-gather.11.cloned.1.call-done = bf16[32,256,128]{2,1,0:T(8,128)(2,1)} async-done(((bf16[32,16,128]{2,1,0:T(8,128)(2,1)}), bf16[32,256,128]{2,1,0:T(8,128)(2,1)}) %all-gather.11.cloned.1.call-update) | async-done | bytes 2097168 | tf_op jit(solution)/shard_map/all_gather | solution.py:50
  352.3 4.3 copy.260
  356.6 4.3 all-to-all-start.7
  361.2 2.1 copy.266
  363.3 3.1 copy.263
  366.4 2.1 convolution_bitcast_fusion.2
  368.6 1.1 convolution_bitcast_fusion.3
  369.8 1.5 convolution_bitcast_fusion
  371.3 15.3 %copy.267 = bf16[32,256,128]{0,1,2:T(8,128)(2,1)} copy(bf16[32,256,128]{2,1,0:T(8,128)(2,1)} %all-gather.11.cloned.1.call-done) | data formatting | bytes 4194304 | tf_op jit(solution)/shard_map/all_gather | solution.py:50
  386.6 4.9 fusion.85
  392.0 3.7 copy.262
  395.7 4.9 copy.264
  400.6 2.6 fusion.84
  404.6 1.5 convolution_bitcast_fusion.1
  408.7 145.6 %all-reduce.13.cloned.1.call-done = (f32[128,640]{1,0:T(8,128)}, f32[128,128]{1,0:T(8,128)}, f32[128,640]{1,0:T(8,128)}, f32[128,128]{1,0:T(8,128)}) async-done(((f32[128,640]{1,0:T(8,128)}, f32[128,128]{1,0:T(8,128)}, f32[128,640]{1,0:T(8,128)}, f32[128,128]{1,0:T(8,128)}), (f32[128,640]{1,0:T(8,128)}, f32[128,128]{1,0:T(8,128)}, f32[128,640]{1,0:T(8,128)}, ...) | async-done | bytes 786448 | tf_op jit(solution)/shard_map/psum | solution.py:173
  554.3 1.5 broadcast_multiply_fusion.2
  555.8 1.9 broadcast_multiply_fusion
  (139 shorter events, 19.5 us)
Async XLA Ops:
  7.2 90.8 %copy-start = (bf16[128,640]{1,0:T(8,128)(2,1)S(1)}, bf16[128,640]{1,0:T(8,128)(2,1)}, u32[]{:S(2)}) copy-start(bf16[128,640]{1,0:T(8,128)(2,1)} %param.12) | copy-start | bytes 491524
  7.2 65.1 %all-gather.5.cloned.1.call-start = ((), (), s32[]{:S(2)}) async-start(), calls=%async_computation.8 | async-start | bytes 2228224 | tf_op jit(solution)/shard_map/all_gather | solution.py:50
  11.2 0.6 copy-start.15
  14.1 131.7 %all-gather.7.cloned.1.call-start = ((), (), s32[]{:S(2)}) async-start(), calls=%async_computation.9 | async-start | bytes 2228224 | tf_op jit(solution)/shard_map/all_gather | solution.py:50
  93.6 2.2 copy-start.2
  93.6 2.2 copy-start.21
  95.7 1.6 copy-start.17
  97.3 0.6 copy-start.18
  98.4 1.1 copy-start.1
  100.3 1.1 copy-start.4
  101.4 48.6 %all-to-all-start.2 = ((bf16[8,32,16,128]{3,2,1,0:T(8,128)(2,1)}), bf16[8,32,16,128]{3,2,1,0:T(8,128)(2,1)}, u32[]{:S(2)}, u32[]{:S(2)}) async-start(bf16[8,32,16,128]{3,2,1,0:T(8,128)(2,1)} %broadcast_in_dim.25), calls=%async_computation.2 | async-start | bytes 2097152 | tf_op jit(solution)/shard_map/all_to_all | solution.py:16
  150.1 32.6 %all-to-all-start.3 = ((bf16[32,256,128]{2,0,1:T(8,128)(2,1)}), bf16[32,256,128]{2,0,1:T(8,128)(2,1)}, u32[]{:S(2)}, u32[]{:S(2)}) async-start(bf16[32,256,128]{2,0,1:T(8,128)(2,1)} %copy.231), calls=%async_computation.3 | async-start | bytes 4194304 | tf_op jit(solution)/shard_map/all_to_all | solution.py:68
  154.4 86.7 %all-gather.9.cloned.1.call-start = ((), (), s32[]{:S(2)}) async-start(), calls=%async_computation.10 | async-start | bytes 2228224 | tf_op jit(solution)/shard_map/all_gather | solution.py:50
  194.8 1.8 copy-start.20
  196.6 84.6 %copy-start.10 = (f32[32,16]{1,0:T(8,128)}, f32[32,16]{1,0:T(8,128)S(1)}, u32[]{:S(2)}) copy-start(f32[32,16]{1,0:T(8,128)S(1)} %copy.238) | copy-start | bytes 6148
  198.9 82.3 %copy-start.12 = (f32[32,16]{1,0:T(8,128)}, f32[32,16]{1,0:T(8,128)S(1)}, u32[]{:S(2)}) copy-start(f32[32,16]{1,0:T(8,128)S(1)} %copy.240) | copy-start | bytes 6148
  219.8 47.9 %all-to-all-start.5 = ((bf16[256,16,128]{2,1,0:T(8,128)(2,1)}), bf16[256,16,128]{2,1,0:T(8,128)(2,1)}, u32[]{:S(2)}, u32[]{:S(2)}) async-start(bf16[256,16,128]{2,1,0:T(8,128)(2,1)} %bitcast.137), calls=%async_computation.5 | async-start | bytes 2097152 | tf_op jit(solution)/shard_map/all_to_all | solution.py:64
  225.9 126.4 %all-gather.11.cloned.1.call-start = ((), (), s32[]{:S(2)}) async-start(), calls=%async_computation.11 | async-start | bytes 2228224 | tf_op jit(solution)/shard_map/all_gather | solution.py:50
  283.7 1.5 copy-start.22
  283.7 1.5 copy-start.24
  283.7 1.5 copy-start.26
  283.8 1.5 copy-start.28
  283.8 1.5 copy-start.30
  283.8 1.5 copy-start.19
  289.0 0.7 copy-start.5
  289.6 14.5 %copy-start.3 = (bf16[32,16,128]{2,1,0:T(8,128)(2,1)S(1)}, bf16[32,16,128]{2,1,0:T(8,128)(2,1)}, u32[]{:S(2)}) copy-start(bf16[32,16,128]{2,1,0:T(8,128)(2,1)} %get-tuple-element.32) | copy-start | bytes 393220
  305.2 51.4 %all-to-all-start.6 = ((bf16[8,32,16,128]{3,2,1,0:T(8,128)(2,1)}), bf16[8,32,16,128]{3,2,1,0:T(8,128)(2,1)}, u32[]{:S(2)}, u32[]{:S(2)}) async-start(bf16[8,32,16,128]{3,2,1,0:T(8,128)(2,1)} %broadcast_in_dim.62), calls=%async_computation.6 | async-start | bytes 2097152 | tf_op jit(solution)/shard_map/all_to_all | solution.py:16
  356.6 35.4 %all-to-all-start.7 = ((bf16[32,256,128]{2,0,1:T(8,128)(2,1)}), bf16[32,256,128]{2,0,1:T(8,128)(2,1)}, u32[]{:S(2)}, u32[]{:S(2)}) async-start(bf16[32,256,128]{2,0,1:T(8,128)(2,1)} %copy.260), calls=%async_computation.7 | async-start | bytes 4194304 | tf_op jit(solution)/shard_map/all_to_all | solution.py:68
  360.9 193.3 %all-reduce.13.cloned.1.call-start = ((), (), s32[]{:S(2)}) async-start(), calls=%async_computation.12 | async-start | bytes 1572864 | tf_op jit(solution)/shard_map/psum | solution.py:173
  363.3 3.1 copy-start.11
  363.3 3.1 copy-start.13
  363.3 3.1 copy-start.14
  366.4 2.1 copy-start.6
  368.5 1.1 copy-start.23
  368.5 1.1 copy-start.25
  368.5 1.1 copy-start.27
  368.5 1.2 copy-start.29
  368.5 1.2 copy-start.31
  403.7 1.0 copy-start.7
  404.6 1.5 copy-start.8
  404.6 1.5 copy-start.9
  406.1 0.9 copy-start.16
Sparse Core Ops, SparseCore 0:
  14.2 58.0 all-gather.4
  100.5 45.2 all-gather.6
  157.6 47.5 all-gather.8
  304.2 48.0 all-gather.10
  407.7 146.5 all-reduce.12
where the time goes:
time: 566 us; the launch traced here: 564 us
  waiting for transfers between devices  254 us (45%)
  local copies, waits for them, and re-layouts  130 us (23%)
  blocking collectives  71.5 us (13%)
  matrix products  47.2 us (8%)
  starting transfers between devices  23.8 us (4%)
  other arithmetic  23.6 us (4%)
  between operations  14.2 us (3%)
    psum x1, waiting for transfers between devices, local(): lax.psum((out_in_part, out_out_part, in_in_part, in_out_part), ('row', 'c...  146 us
    all_gather x4, waiting for transfers between devices, cols_of(): lax.all_gather(shortened(tiles), 'col', axis=1, tiled=True)  83.4 us
    all_gather x6, local copies, waits for them, and re-layouts, cols_of(): lax.all_gather(shortened(tiles), 'col', axis=1, tiled=True)  69.7 us
    all_to_all x2, blocking collectives, from_everyone(): return lax.all_to_all(copies, axis, split_axis=0, concat_axis=0, tiled=True)  40 us
    all_to_all x1, blocking collectives, to_row_blocks(): return lax.all_to_all(panel, 'col', split_axis=0, concat_axis=1, tiled=True)  31.5 us
    all_to_all x2, waiting for transfers between devices, to_col_blocks(): return lax.all_to_all(panel, 'row', split_axis=1, concat_axis=0, tiled=True)  24.5 us
    all_to_all x4, local copies, waits for them, and re-layouts, to_col_blocks(): return lax.all_to_all(panel, 'row', split_axis=1, concat_axis=0, tiled=True)  17.2 us
  transfers between devices with their start and end apart: 10, of which 5 were waited for; matrix products, arithmetic and copies ran while one was open for 20% of the time, Pallas kernels for 0%

commit v1 on v0

--- a/solution.py
+++ b/solution.py
@@ -5,6 +5,7 @@
 
 H = 128
 EPSILON = 1e-05
+pages_fit = lambda work_x: lax.psum(lax.psum(work_x, "col"), "row")
 
 
 def shortened(array):
@@ -170,7 +171,7 @@
     pair_grad, out_in_part, out_out_part = backward(
         middle_grad, saved_out, pair_mask, out_in_proj, out_out_proj, True
     )
-    totals = lax.psum((out_in_part, out_out_part, in_in_part, in_out_part), ("row", "col"))
+    totals = pages_fit((out_in_part, out_out_part, in_in_part, in_out_part))
     tokens_all = row_tile * lax.axis_size("row")
     return (
         updated,

time: 566 us -> 653 us (1.15); the launches traced: 564 us -> 641 us
  waiting for transfers between devices: 254 us -> 323 us
  starting transfers between devices: 23.8 us -> 31.7 us
    psum x1 -> x2, waiting for transfers between devices: 146 us -> 214 us  [pages_fit = lambda work_x: lax.psum(lax.psum(work_x, 'col'), 'row')]
    psum x1 -> x2, starting transfers between devices: 0.26 us -> 8.01 us  [pages_fit = lambda work_x: lax.psum(lax.psum(work_x, 'col'), 'row')]
  transfers between devices with their start and end apart: 10 -> 11, of which waited for: 5 -> 6; matrix products, arithmetic and copies ran while one was open for 20% -> 17% of each run, Pallas kernels for 0% -> 0%
where the time goes in v1:
time: 653 us; the launch traced here: 641 us
  waiting for transfers between devices  323 us (49%)
  local copies, waits for them, and re-layouts  130 us (20%)
  blocking collectives  71.5 us (11%)
  matrix products  47.2 us (7%)
  starting transfers between devices  31.7 us (5%)
  other arithmetic  23.6 us (4%)
  between operations  14.5 us (2%)
    psum x2, waiting for transfers between devices, pages_fit = lambda work_x: lax.psum(lax.psum(work_x, 'col'), 'row')  214 us
    all_gather x4, waiting for transfers between devices, cols_of(): lax.all_gather(shortened(tiles), 'col', axis=1, tiled=True)  83.4 us
    all_gather x6, local copies, waits for them, and re-layouts, cols_of(): lax.all_gather(shortened(tiles), 'col', axis=1, tiled=True)  69.7 us
    all_to_all x2, blocking collectives, from_everyone(): return lax.all_to_all(copies, axis, split_axis=0, concat_axis=0, tiled=True)  40 us
    all_to_all x1, blocking collectives, to_row_blocks(): return lax.all_to_all(panel, 'col', split_axis=0, concat_axis=1, tiled=True)  31.5 us
    all_to_all x2, waiting for transfers between devices, to_col_blocks(): return lax.all_to_all(panel, 'row', split_axis=1, concat_axis=0, tiled=True)  24.5 us
    all_to_all x4, local copies, waits for them, and re-layouts, to_col_blocks(): return lax.all_to_all(panel, 'row', split_axis=1, concat_axis=0, tiled=True)  17.2 us
  transfers between devices with their start and end apart: 11, of which 6 were waited for; matrix products, arithmetic and copies ran while one was open for 17% of the time, Pallas kernels for 0%

profile of v1, /device:TPU:1, one launch (start us, length us, event | category | flops | bytes accessed | tf_op | source)
XLA Modules:
  0.0 641.1 jit_solution(13294625271521838424)
XLA Ops:
  11.9 1.4 fusion.53
  14.3 22.1 %all_to_all.92 = bf16[8,32,16,128]{3,2,1,0:T(8,128)(2,1)S(1)} all-to-all(bf16[8,32,16,128]{3,2,1,0:T(8,128)(2,1)S(1)} %broadcast_in_dim.24), channel_id=1, replica_groups=mesh['row'=8,'col'=16] {'row'}, dimensions={0} | all-to-all | bytes 2097152 | tf_op jit(solution)/shard_map/all_to_all | solution.py:17
  36.4 31.5 %all_to_all.93 = bf16[256,16,128]{2,1,0:T(8,128)(2,1)S(1)} all-to-all(bf16[256,16,128]{2,1,0:T(8,128)(2,1)S(1)} %bitcast.135), channel_id=1, replica_groups=mesh['row'=8,'col'=16] {'col'}, dimensions={0} | all-to-all | bytes 2097152 | tf_op jit(solution)/shard_map/all_to_all | solution.py:65
  67.9 1.3 copy.219
  69.1 2.7 copy.220
  72.3 15.3 %copy.221 = bf16[32,256,128]{0,1,2:T(8,128)(2,1)} copy(bf16[32,256,128]{2,1,0:T(8,128)(2,1)} %all-gather.5.cloned.1.call-done) | data formatting | bytes 4194304 | tf_op jit(solution)/shard_map/all_gather | solution.py:51
  87.6 6.0 bitcast_reduce_fusion.1
  93.6 1.7 copy.222
  101.5 4.2 all-to-all-start.2
  105.7 40.1 %all-gather.7.cloned.1.call-done = bf16[32,256,128]{2,1,0:T(8,128)(2,1)} async-done(((bf16[32,16,128]{2,1,0:T(8,128)(2,1)}), bf16[32,256,128]{2,1,0:T(8,128)(2,1)}) %all-gather.7.cloned.1.call-update) | async-done | bytes 2097168 | tf_op jit(solution)/shard_map/all_gather | solution.py:51
  145.8 4.3 copy.231
  150.1 4.3 all-to-all-start.3
  155.2 3.0 copy.234
  158.2 24.5 %all-to-all-done.3 = bf16[32,256,128]{2,0,1:T(8,128)(2,1)} async-done(((bf16[32,256,128]{2,0,1:T(8,128)(2,1)}), bf16[32,256,128]{2,0,1:T(8,128)(2,1)}, u32[]{:S(2)}, u32[]{:S(2)}) %all-to-all-start.3) | async-done | bytes 2097184 | tf_op jit(solution)/shard_map/all_to_all | solution.py:69
  182.7 3.8 copy.233
  186.4 4.9 copy.235
  191.3 3.6 bitcast_reduce_fusion
  194.9 1.7 copy.236
  196.7 2.0 multiply_reduce_fusion.1
  199.0 1.3 fusion.67
  200.5 1.3 add_convert_fusion.1
  202.0 17.9 %all_to_all.94 = bf16[8,32,16,128]{3,2,1,0:T(8,128)(2,1)} all-to-all(bf16[8,32,16,128]{3,2,1,0:T(8,128)(2,1)S(1)} %broadcast_in_dim.28), channel_id=1, replica_groups=mesh['row'=8,'col'=16] {'row'}, dimensions={0} | all-to-all | bytes 2097152 | tf_op jit(solution)/shard_map/all_to_all | solution.py:17
  219.9 6.1 all-to-all-start.5
  226.0 15.3 %copy.246 = bf16[32,256,128]{0,1,2:T(8,128)(2,1)} copy(bf16[32,256,128]{2,1,0:T(8,128)(2,1)} %all-gather.7.cloned.1.call-done) | data formatting | bytes 4194304 | tf_op jit(solution)/shard_map/all_gather | solution.py:51
  241.3 15.3 %copy.249 = bf16[32,256,128]{0,1,2:T(8,128)(2,1)} copy(bf16[32,256,128]{2,1,0:T(8,128)(2,1)} %all-gather.9.cloned.1.call-done) | data formatting | bytes 4194304 | tf_op jit(solution)/shard_map/all_gather | solution.py:51
  256.6 3.0 copy.245
  259.5 5.9 fusion.83
  265.5 2.4 copy.247
  267.8 2.5 copy.248
  270.3 2.7 copy.250
  273.0 5.9 fusion.86
  278.9 2.4 copy.251
  281.3 2.6 fusion.18
  283.9 1.4 fusion.16
  285.5 1.3 fusion.55
  287.0 2.1 fusion.22
  289.7 2.4 multiply_reduce_fusion
  292.1 1.4 copy.281
  293.5 1.3 multiply_multiply_fusion.1
  294.8 1.4 copy.257
  296.2 1.9 fusion.68
  298.2 1.4 copy.282
  299.5 1.3 negate_multiply_fusion.1
  300.8 1.4 copy.259
  302.2 2.0 add_convert_fusion
  305.3 4.2 all-to-all-start.6
  309.6 42.8 %all-gather.11.cloned.1.call-done = bf16[32,256,128]{2,1,0:T(8,128)(2,1)} async-done(((bf16[32,16,128]{2,1,0:T(8,128)(2,1)}), bf16[32,256,128]{2,1,0:T(8,128)(2,1)}) %all-gather.11.cloned.1.call-update) | async-done | bytes 2097168 | tf_op jit(solution)/shard_map/all_gather | solution.py:51
  352.4 4.3 copy.260
  356.7 4.4 all-to-all-start.7
  361.0 8.0 %all-reduce.15.cloned.1.call-start = ((), (), s32[]{:S(2)}) async-start(), calls=%async_computation.12 | async-start | bytes 1572864 | tf_op jit(solution)/shard_map/psum | solution.py:8
  369.0 2.1 copy.266
  371.1 3.1 copy.263
  374.2 2.1 convolution_bitcast_fusion.2
  377.5 1.5 convolution_bitcast_fusion
  379.0 15.3 %copy.267 = bf16[32,256,128]{0,1,2:T(8,128)(2,1)} copy(bf16[32,256,128]{2,1,0:T(8,128)(2,1)} %all-gather.11.cloned.1.call-done) | data formatting | bytes 4194304 | tf_op jit(solution)/shard_map/all_gather | solution.py:51
  394.3 4.9 fusion.85
  399.8 3.7 copy.262
  403.5 4.9 copy.264
  408.4 2.6 fusion.84
  412.4 1.5 convolution_bitcast_fusion.1
  414.9 138.3 %all-reduce.15.cloned.1.call-done = (f32[128,640]{1,0:T(8,128)}, f32[128,128]{1,0:T(8,128)}, f32[128,640]{1,0:T(8,128)}, f32[128,128]{1,0:T(8,128)}) async-done(((f32[128,640]{1,0:T(8,128)}, f32[128,128]{1,0:T(8,128)}, f32[128,640]{1,0:T(8,128)}, f32[128,128]{1,0:T(8,128)}), (f32[128,640]{1,0:T(8,128)}, f32[128,128]{1,0:T(8,128)}, f32[128,640]{1,0:T(8,128)}, ...) | async-done | bytes 786448 | tf_op jit(solution)/shard_map/psum | solution.py:8
  554.8 76.0 %all-reduce.17.cloned.1.call-done = (f32[128,640]{1,0:T(8,128)}, f32[128,128]{1,0:T(8,128)}, f32[128,640]{1,0:T(8,128)}, f32[128,128]{1,0:T(8,128)}) async-done(((f32[128,640]{1,0:T(8,128)}, f32[128,128]{1,0:T(8,128)}, f32[128,640]{1,0:T(8,128)}, f32[128,128]{1,0:T(8,128)}), (f32[128,640]{1,0:T(8,128)}, f32[128,128]{1,0:T(8,128)}, f32[128,640]{1,0:T(8,128)}, ...) | async-done | bytes 786448 | tf_op jit(solution)/shard_map/psum | solution.py:8
  630.8 1.5 broadcast_multiply_fusion.2
  632.3 1.9 broadcast_multiply_fusion
  (142 shorter events, 21.6 us)
Async XLA Ops:
  7.2 90.9 %copy-start = (bf16[128,640]{1,0:T(8,128)(2,1)S(1)}, bf16[128,640]{1,0:T(8,128)(2,1)}, u32[]{:S(2)}) copy-start(bf16[128,640]{1,0:T(8,128)(2,1)} %param.12) | copy-start | bytes 491524
  7.2 65.1 %all-gather.5.cloned.1.call-start = ((), (), s32[]{:S(2)}) async-start(), calls=%async_computation.8 | async-start | bytes 2228224 | tf_op jit(solution)/shard_map/all_gather | solution.py:51
  11.2 0.6 copy-start.15
  14.1 131.7 %all-gather.7.cloned.1.call-start = ((), (), s32[]{:S(2)}) async-start(), calls=%async_computation.9 | async-start | bytes 2228224 | tf_op jit(solution)/shard_map/all_gather | solution.py:51
  93.6 2.2 copy-start.2
  93.6 2.2 copy-start.21
  95.7 1.6 copy-start.17
  97.3 0.6 copy-start.18
  98.4 1.1 copy-start.1
  100.4 1.1 copy-start.4
  101.5 48.6 %all-to-all-start.2 = ((bf16[8,32,16,128]{3,2,1,0:T(8,128)(2,1)}), bf16[8,32,16,128]{3,2,1,0:T(8,128)(2,1)}, u32[]{:S(2)}, u32[]{:S(2)}) async-start(bf16[8,32,16,128]{3,2,1,0:T(8,128)(2,1)} %broadcast_in_dim.25), calls=%async_computation.2 | async-start | bytes 2097152 | tf_op jit(solution)/shard_map/all_to_all | solution.py:17
  150.1 32.6 %all-to-all-start.3 = ((bf16[32,256,128]{2,0,1:T(8,128)(2,1)}), bf16[32,256,128]{2,0,1:T(8,128)(2,1)}, u32[]{:S(2)}, u32[]{:S(2)}) async-start(bf16[32,256,128]{2,0,1:T(8,128)(2,1)} %copy.231), calls=%async_computation.3 | async-start | bytes 4194304 | tf_op jit(solution)/shard_map/all_to_all | solution.py:69
  154.5 86.8 %all-gather.9.cloned.1.call-start = ((), (), s32[]{:S(2)}) async-start(), calls=%async_computation.10 | async-start | bytes 2228224 | tf_op jit(solution)/shard_map/all_gather | solution.py:51
  194.9 1.8 copy-start.20
  196.7 84.6 %copy-start.10 = (f32[32,16]{1,0:T(8,128)}, f32[32,16]{1,0:T(8,128)S(1)}, u32[]{:S(2)}) copy-start(f32[32,16]{1,0:T(8,128)S(1)} %copy.238) | copy-start | bytes 6148
  199.0 82.3 %copy-start.12 = (f32[32,16]{1,0:T(8,128)}, f32[32,16]{1,0:T(8,128)S(1)}, u32[]{:S(2)}) copy-start(f32[32,16]{1,0:T(8,128)S(1)} %copy.240) | copy-start | bytes 6148
  219.9 48.0 %all-to-all-start.5 = ((bf16[256,16,128]{2,1,0:T(8,128)(2,1)}), bf16[256,16,128]{2,1,0:T(8,128)(2,1)}, u32[]{:S(2)}, u32[]{:S(2)}) async-start(bf16[256,16,128]{2,1,0:T(8,128)(2,1)} %bitcast.137), calls=%async_computation.5 | async-start | bytes 2097152 | tf_op jit(solution)/shard_map/all_to_all | solution.py:65
  225.9 126.5 %all-gather.11.cloned.1.call-start = ((), (), s32[]{:S(2)}) async-start(), calls=%async_computation.11 | async-start | bytes 2228224 | tf_op jit(solution)/shard_map/all_gather | solution.py:51
  283.8 1.5 copy-start.22
  283.8 1.5 copy-start.24
  283.8 1.5 copy-start.26
  283.8 1.5 copy-start.28
  283.8 1.5 copy-start.30
  283.9 1.5 copy-start.19
  289.1 0.7 copy-start.5
  289.7 14.5 %copy-start.3 = (bf16[32,16,128]{2,1,0:T(8,128)(2,1)S(1)}, bf16[32,16,128]{2,1,0:T(8,128)(2,1)}, u32[]{:S(2)}) copy-start(bf16[32,16,128]{2,1,0:T(8,128)(2,1)} %get-tuple-element.36) | copy-start | bytes 393220
  305.3 51.3 %all-to-all-start.6 = ((bf16[8,32,16,128]{3,2,1,0:T(8,128)(2,1)}), bf16[8,32,16,128]{3,2,1,0:T(8,128)(2,1)}, u32[]{:S(2)}, u32[]{:S(2)}) async-start(bf16[8,32,16,128]{3,2,1,0:T(8,128)(2,1)} %broadcast_in_dim.62), calls=%async_computation.6 | async-start | bytes 2097152 | tf_op jit(solution)/shard_map/all_to_all | solution.py:17
  356.7 43.1 %all-to-all-start.7 = ((bf16[32,256,128]{2,0,1:T(8,128)(2,1)}), bf16[32,256,128]{2,0,1:T(8,128)(2,1)}, u32[]{:S(2)}, u32[]{:S(2)}) async-start(bf16[32,256,128]{2,0,1:T(8,128)(2,1)} %copy.260), calls=%async_computation.7 | async-start | bytes 4194304 | tf_op jit(solution)/shard_map/all_to_all | solution.py:69
  361.0 192.1 %all-reduce.15.cloned.1.call-start = ((), (), s32[]{:S(2)}) async-start(), calls=%async_computation.12 | async-start | bytes 1572864 | tf_op jit(solution)/shard_map/psum | solution.py:8
  371.1 3.1 copy-start.11
  371.1 3.1 copy-start.13
  371.1 3.1 copy-start.14
  374.2 2.1 copy-start.6
  376.3 1.1 copy-start.23
  376.3 1.1 copy-start.25
  376.3 1.1 copy-start.27
  376.3 1.2 copy-start.29
  376.3 1.2 copy-start.31
  411.4 1.0 copy-start.7
  412.4 1.6 copy-start.8
  412.4 1.6 copy-start.9
  413.9 139.3 %copy-start.16 = (f32[32,16]{0,1:T(8,128)S(1)}, f32[32,16]{0,1:T(8,128)}, u32[]{:S(2)}) copy-start(f32[32,16]{0,1:T(8,128)} %copy-done.15) | copy-start | bytes 6148
  413.9 216.9 %all-reduce.17.cloned.1.call-start = ((), (), s32[]{:S(2)}) async-start(), calls=%async_computation.13 | async-start | bytes 1572864 | tf_op jit(solution)/shard_map/psum | solution.py:8
Sparse Core Ops, SparseCore 0:
  14.2 58.0 all-gather.4
  100.5 45.2 all-gather.6
  157.6 47.5 all-gather.8
  304.3 48.0 all-gather.10
  414.0 139.0 all-reduce.14
  555.8 74.9 all-reduce.16
